TPU v7x, 256 devices: a whole 4x4x8 slice. The times are simulated.
256 devices in a mesh: slab: 64 (over y, x_hi, z), sub: 4 (over x_lo, core).
Axes of the slice: x: 4 (x_hi: 2, x_lo: 2; x = x_hi * 2 + x_lo), y: 4, z: 8, core: 2. Of those that a mesh axis runs over, the one named last changes fastest.
Arguments:
- right_sides: bfloat16 [524288, 768], P(('slab', 'sub')), may hold values from -6 to 6
- front_sides: bfloat16 [131072, 768], P(('slab', 'sub')), may hold values from -6 to 6
- pending_front: bfloat16 [131072, 256], P(('slab', 'sub')), may hold values from -6 to 6
- inner_index: int32 [4096, 6], P(('slab', 'sub')), may hold values from 0 to 15, all different within a row
- inner_blocks: bfloat16 [4096, 6, 128, 128], P(('slab', 'sub')), may hold values from -0.15625 to 0.15625
- inner_inverse: bfloat16 [4096, 128, 128], P(('slab', 'sub')), may hold values from -1 to 2
- outer_index: int32 [1024, 8], P(('slab', 'sub')), may hold values from 0 to 15, all different within a row
- outer_blocks: bfloat16 [1024, 8, 128, 128], P(('slab', 'sub')), may hold values from -0.125 to 0.125
- front_inverse: bfloat16 [1024, 128, 128], P(('slab', 'sub')), may hold values from -1 to 2
Outputs:
- solution: bfloat16 [524288, 768], P(('slab', 'sub'))
- front_solution: bfloat16 [131072, 768], P(('slab', 'sub'))
All inputs are finite; a program needn't handle non-finite values.
Results may differ from a plain program's by a relative error of at most 0.009.
Values may be sent and summed in bfloat16 or wider, within the bound.
A program may use at most 64 MiB of HBM per device.

v0:
```python
import jax
import jax.numpy as jnp
from jax import lax
from jax.sharding import PartitionSpec as P


def passed_along(x, axis, by):
    size = lax.axis_size(axis)
    pairs = [(i, i + by) for i in range(size) if 0 <= i + by < size]
    return lax.ppermute(x, axis, pairs)


def collect(share):
    return lax.all_gather(share, "sub", axis=0, tiled=True)


def shards(
    right_sides,
    front_sides,
    pending_front,
    inner_index,
    inner_blocks,
    inner_inverse,
    outer_index,
    outer_blocks,
    front_inverse,
):
    block_size = inner_inverse.shape[1]
    inner_rows = inner_inverse.shape[0]
    outer_rows = front_inverse.shape[0]
    columns = pending_front.shape[1]
    groups = right_sides.shape[1] // columns
    gathered = collect(pending_front)
    solved_list = []
    front_list = []
    for group in range(groups):
        front_blocks = gathered.reshape(-1, block_size, columns)
        picked = jnp.take(front_blocks, inner_index, axis=0)
        coupled = jnp.einsum(
            "ikab,ikbc->iac", inner_blocks, picked, preferred_element_type=jnp.float32
        )
        group_sides = right_sides[:, group * columns : (group + 1) * columns].reshape(
            inner_rows, block_size, columns
        )
        inner_values = (group_sides.astype(jnp.float32) - coupled).astype(jnp.bfloat16)
        solved = jnp.einsum(
            "iab,ibc->iac", inner_inverse, inner_values, preferred_element_type=jnp.float32
        ).astype(jnp.bfloat16)
        chosen = jnp.take(solved, outer_index, axis=0)
        outgoing = jnp.einsum(
            "jkab,jkbc->jac", outer_blocks, chosen, preferred_element_type=jnp.float32
        )
        outer_sides = front_sides[:, group * columns : (group + 1) * columns].reshape(
            outer_rows, block_size, columns
        )
        outer_values = (outer_sides.astype(jnp.float32) - outgoing).astype(jnp.bfloat16)
        front_done = jnp.einsum(
            "jab,jbc->jac", front_inverse, outer_values, preferred_element_type=jnp.float32
        ).astype(jnp.bfloat16)
        front_done = front_done.reshape(-1, columns)
        solved_list.append(solved.reshape(-1, columns))
        front_list.append(front_done)
        if group + 1 < groups:
            gathered = passed_along(collect(front_done), "slab", 1)
    solution = jnp.concatenate(solved_list, axis=1)
    front_solution = jnp.concatenate(front_list, axis=1)
    return (solution, front_solution)


def solution(mesh):
    placed = (
        P(("slab", "sub"), None),
        P(("slab", "sub"), None),
        P(("slab", "sub"), None),
        P(("slab", "sub"), None),
        P(("slab", "sub"), None, None, None),
        P(("slab", "sub"), None, None),
        P(("slab", "sub"), None),
        P(("slab", "sub"), None, None, None),
        P(("slab", "sub"), None, None),
    )
    return jax.shard_map(
        shards,
        mesh=mesh,
        in_specs=placed,
        out_specs=(P(("slab", "sub"), None), P(("slab", "sub"), None)),
        check_vma=False,
    )
```

profile of v0, /device:TPU:9, one launch (start us, length us, event | category | flops | bytes accessed | tf_op | source)
XLA Modules:
  0.0 216.6 jit_solution(2010275956903110285)
XLA Ops:
  7.2 0.7 all-gather.4.cloned.1.call-update
  8.0 0.8 compare_and_fusion
  8.8 0.7 compare_select_fusion.1
  9.5 0.1 copy.17
  9.6 0.1 reshape.138
  9.7 0.7 compare_select_fusion
  10.4 0.1 copy.18
  10.5 0.1 reshape.134
  10.6 0.7 compare_and_fusion.1
  11.3 2.0 fusion.115
  13.2 3.6 %fusion.114 = (bf16[2048,256]{1,0:T(8,128)(2,1)}, bf16[2048,256]{1,0:T(8,128)(2,1)}, bf16[2048,256]{1,0:T(8,128)(2,1)}) fusion(bf16[2048,768]{1,0:T(8,128)(2,1)} %param.13), kind=kLoop, calls=%fused_computation.74 | loop fusion | bytes 6291456 | tf_op jit(solution)/shard_map/slice | solution.py:42
  16.8 19.5 %all-gather.4.cloned.1.call-done = bf16[2048,256]{1,0:T(8,128)(2,1)} async-done(((bf16[512,256]{1,0:T(8,128)(2,1)}), bf16[2048,256]{1,0:T(8,128)(2,1)}) %all-gather.4.cloned.1.call-update) | async-done | bytes 1048592 | tf_op jit(solution)/shard_map/all_gather | solution.py:14
  36.3 7.2 %gather_fusion = bf16[96,128,256]{2,1,0:T(8,128)(2,1)} fusion(bf16[16,128,256]{2,1,0:T(8,128)(2,1)} %bitcast.123, s32[1024]{0:T(1024)S(1)} %pad_clamp_fusion.1), kind=kCustom, calls=%fused_computation.clone | custom fusion | bytes 12583296 | tf_op jit(solution)/shard_map/jit(_take)/gather | solution.py:38
  43.5 6.0 %fusion.45 = bf16[16,256,128]{1,2,0:T(8,128)(2,1)} fusion(bf16[16,128,128]{2,1,0:T(8,128)(2,1)} %param.18, bf16[16,128,256]{2,1,0:T(8,128)(2,1)} %bitcast.142, bf16[16,6,128,128]{3,2,1,0:T(8,128)(2,1)S(1)} %copy-done, bf16[16,6,128,256]{3,2,1,0:T(8,128)(2,1)} %bitcast.131, pred[16,6]{1,0:T(8,128)(4,1)S(1)} %copy.17), kind=kOutput, calls=%fused_computation.39 | convolution fusion | flops 944766976 | bytes 12058720 | tf_op jit(solution)/shard_map/iab,ibc->iac/dot_general | solution.py:46
  49.6 3.3 %gather_fusion.1 = bf16[32,128,256]{2,1,0:T(8,128)(2,1)} fusion(bf16[16,128,256]{2,1,0:T(8,128)(2,1)} %bitcast.124, s32[1024]{0:T(1024)S(1)} %pad_clamp_fusion), kind=kCustom, calls=%fused_computation.1.clone | custom fusion | bytes 4194432 | tf_op jit(solution)/shard_map/jit(_take)/gather | solution.py:49
  52.8 3.4 %fusion.90 = bf16[4,256,128]{1,2,0:T(8,128)(2,1)} fusion(bf16[4,128,128]{2,1,0:T(8,128)(2,1)S(1)} %copy-done.2, bf16[4,8,128,128]{3,2,1,0:T(8,128)(2,1)} %param.20, bf16[4,8,128,256]{3,2,1,0:T(8,128)(2,1)} %bitcast.134, pred[4,8]{1,0:T(4,128)(4,1)S(1)} %compare_and_fusion.1, bf16[4,128,256]{2,1,0:T(8,128)(2,1)} %bitcast.145), kind=kOutput, calls=%fused_computation.54 | convolution fusion | flops 303562752 | bytes 3801120 | tf_op jit(solution)/shard_map/jab,jbc->jac/dot_general | solution.py:57
  56.3 24.2 %all-gather.6.cloned.1.call-done = bf16[2048,256]{1,0:T(8,128)(2,1)} async-done(((bf16[512,256]{1,0:T(8,128)(2,1)}), bf16[2048,256]{1,0:T(8,128)(2,1)}) %all-gather.6.cloned.1.call-update) | async-done | bytes 1048592 | tf_op jit(solution)/shard_map/all_gather | solution.py:14
  80.5 3.2 %collective-permute-start = (bf16[2048,256]{1,0:T(8,128)(2,1)}, bf16[2048,256]{1,0:T(8,128)(2,1)}, u32[]{:S(2)}, u32[]{:S(2)}) collective-permute-start(bf16[2048,256]{1,0:T(8,128)(2,1)} %all-gather.6.cloned.1.call-done), channel_id=1, source_target_pairs={{0,4},{4,8},{8,12},{12,16},{16,20},{20,24},{24,28},{28,32},{32,36}... | collective-permute-start | bytes 3145736 | tf_op jit(solution)/shard_map/ppermute | solution.py:10
  83.7 28.4 %collective-permute-done = bf16[2048,256]{1,0:T(8,128)(2,1)} collective-permute-done((bf16[2048,256]{1,0:T(8,128)(2,1)}, bf16[2048,256]{1,0:T(8,128)(2,1)}, u32[]{:S(2)}, u32[]{:S(2)}) %collective-permute-start) | collective-permute-done | bytes 1048608 | tf_op jit(solution)/shard_map/ppermute | solution.py:10
  112.1 7.2 %gather_fusion.2 = bf16[96,128,256]{2,1,0:T(8,128)(2,1)} fusion(bf16[16,128,256]{2,1,0:T(8,128)(2,1)} %bitcast.16, s32[1024]{0:T(1024)S(1)} %pad_clamp_fusion.1), kind=kCustom, calls=%fused_computation.2.clone | custom fusion | bytes 12583296 | tf_op jit(solution)/shard_map/jit(_take)/gather | solution.py:38
  119.3 6.1 %fusion.42 = bf16[16,256,128]{1,2,0:T(8,128)(2,1)} fusion(bf16[16,128,128]{2,1,0:T(8,128)(2,1)} %param.18, bf16[16,128,256]{2,1,0:T(8,128)(2,1)} %bitcast.141, bf16[16,6,128,128]{3,2,1,0:T(8,128)(2,1)S(1)} %copy-done, bf16[16,6,128,256]{3,2,1,0:T(8,128)(2,1)} %bitcast.132, pred[16,6]{1,0:T(8,128)(4,1)S(1)} %copy.17), kind=kOutput, calls=%fused_computation.38 | convolution fusion | flops 944766976 | bytes 12058720 | tf_op jit(solution)/shard_map/iab,ibc->iac/dot_general | solution.py:46
  125.4 3.2 %gather_fusion.3 = bf16[32,128,256]{2,1,0:T(8,128)(2,1)} fusion(bf16[16,128,256]{2,1,0:T(8,128)(2,1)} %bitcast.126, s32[1024]{0:T(1024)S(1)} %pad_clamp_fusion), kind=kCustom, calls=%fused_computation.4.clone | custom fusion | bytes 4194432 | tf_op jit(solution)/shard_map/jit(_take)/gather | solution.py:49
  128.6 3.4 %fusion.87 = bf16[4,256,128]{1,2,0:T(8,128)(2,1)} fusion(bf16[4,128,128]{2,1,0:T(8,128)(2,1)S(1)} %copy-done.2, bf16[4,8,128,128]{3,2,1,0:T(8,128)(2,1)} %param.20, bf16[4,8,128,256]{3,2,1,0:T(8,128)(2,1)} %bitcast.135, pred[4,8]{1,0:T(4,128)(4,1)S(1)} %compare_and_fusion.1, bf16[4,128,256]{2,1,0:T(8,128)(2,1)S(1)} %bitcast.144), kind=kOutput, calls=%fused_computation.53 | convolution fusion | flops 303562752 | bytes 3801120 | tf_op jit(solution)/shard_map/jab,jbc->jac/dot_general | solution.py:57
  132.1 21.4 %all-gather.8.cloned.1.call-done = bf16[2048,256]{1,0:T(8,128)(2,1)} async-done(((bf16[512,256]{1,0:T(8,128)(2,1)}), bf16[2048,256]{1,0:T(8,128)(2,1)}) %all-gather.8.cloned.1.call-update) | async-done | bytes 1048592 | tf_op jit(solution)/shard_map/all_gather | solution.py:14
  153.5 3.4 %collective-permute-start.1 = (bf16[2048,256]{1,0:T(8,128)(2,1)}, bf16[2048,256]{1,0:T(8,128)(2,1)}, u32[]{:S(2)}, u32[]{:S(2)}) collective-permute-start(bf16[2048,256]{1,0:T(8,128)(2,1)} %all-gather.8.cloned.1.call-done), channel_id=1, source_target_pairs={{0,4},{4,8},{8,12},{12,16},{16,20},{20,24},{24,28},{28,32},{32,36}... | collective-permute-start | bytes 3145736 | tf_op jit(solution)/shard_map/ppermute | solution.py:10
  156.9 28.3 %collective-permute-done.1 = bf16[2048,256]{1,0:T(8,128)(2,1)} collective-permute-done((bf16[2048,256]{1,0:T(8,128)(2,1)}, bf16[2048,256]{1,0:T(8,128)(2,1)}, u32[]{:S(2)}, u32[]{:S(2)}) %collective-permute-start.1) | collective-permute-done | bytes 1048608 | tf_op jit(solution)/shard_map/ppermute | solution.py:10
  185.1 7.2 %gather_fusion.4 = bf16[96,128,256]{2,1,0:T(8,128)(2,1)} fusion(bf16[16,128,256]{2,1,0:T(8,128)(2,1)} %bitcast.31, s32[1024]{0:T(1024)S(1)} %pad_clamp_fusion.1), kind=kCustom, calls=%fused_computation.3.clone | custom fusion | bytes 12583296 | tf_op jit(solution)/shard_map/jit(_take)/gather | solution.py:38
  192.3 6.0 %fusion.39 = bf16[16,256,128]{1,2,0:T(8,128)(2,1)} fusion(bf16[16,128,128]{2,1,0:T(8,128)(2,1)} %param.18, bf16[16,128,256]{2,1,0:T(8,128)(2,1)} %bitcast.140, bf16[16,6,128,128]{3,2,1,0:T(8,128)(2,1)S(1)} %copy-done, bf16[16,6,128,256]{3,2,1,0:T(8,128)(2,1)} %bitcast.130, pred[16,6]{1,0:T(8,128)(4,1)S(1)} %copy.17), kind=kOutput, calls=%fused_computation.37 | convolution fusion | flops 944766976 | bytes 12058720 | tf_op jit(solution)/shard_map/iab,ibc->iac/dot_general | solution.py:46
  198.3 3.2 %gather_fusion.5 = bf16[32,128,256]{2,1,0:T(8,128)(2,1)} fusion(bf16[16,128,256]{2,1,0:T(8,128)(2,1)} %bitcast.128, s32[1024]{0:T(1024)S(1)} %pad_clamp_fusion), kind=kCustom, calls=%fused_computation.5.clone | custom fusion | bytes 4194432 | tf_op jit(solution)/shard_map/jit(_take)/gather | solution.py:49
  201.6 3.4 %fusion.84 = bf16[4,256,128]{1,2,0:T(8,128)(2,1)} fusion(bf16[4,128,128]{2,1,0:T(8,128)(2,1)S(1)} %copy-done.2, bf16[4,8,128,128]{3,2,1,0:T(8,128)(2,1)} %param.20, bf16[4,8,128,256]{3,2,1,0:T(8,128)(2,1)} %bitcast.133, pred[4,8]{1,0:T(4,128)(4,1)S(1)} %compare_and_fusion.1, bf16[4,128,256]{2,1,0:T(8,128)(2,1)} %bitcast.143), kind=kOutput, calls=%fused_computation.52 | convolution fusion | flops 303562752 | bytes 3801120 | tf_op jit(solution)/shard_map/jab,jbc->jac/dot_general | solution.py:57
  205.0 2.0 pad_maximum_fusion.1
  206.9 3.1 %pad_maximum_fusion = bf16[2048,768]{1,0:T(8,128)(2,1)} fusion(bf16[2048,256]{1,0:T(8,128)(2,1)} %bitcast.129, bf16[2048,256]{1,0:T(8,128)(2,1)} %bitcast.127, bf16[2048,256]{1,0:T(8,128)(2,1)} %bitcast.125), kind=kLoop, calls=%fused_computation.15 | loop fusion | flops 9437184 | bytes 6291456 | tf_op jit(solution)/shard_map/concatenate | solution.py:65
  (13 shorter events, 0.2 us)
Async XLA Ops:
  7.2 36.4 %copy-start = (bf16[16,6,128,128]{3,2,1,0:T(8,128)(2,1)S(1)}, bf16[16,6,128,128]{3,2,1,0:T(8,128)(2,1)}, u32[]{:S(2)}) copy-start(bf16[16,6,128,128]{3,2,1,0:T(8,128)(2,1)} %param.17) | copy-start | bytes 9437188
  7.2 29.1 %all-gather.4.cloned.1.call-start = ((), (), s32[]{:S(2)}) async-start(), calls=%async_computation | async-start | bytes 1310720 | tf_op jit(solution)/shard_map/all_gather | solution.py:14
  7.9 72.6 %all-gather.6.cloned.1.call-start = ((), (), s32[]{:S(2)}) async-start(), calls=%async_computation.1 | async-start | bytes 1310720 | tf_op jit(solution)/shard_map/all_gather | solution.py:14
  49.6 3.3 %copy-start.2 = (bf16[4,128,128]{2,1,0:T(8,128)(2,1)S(1)}, bf16[4,128,128]{2,1,0:T(8,128)(2,1)}, u32[]{:S(2)}) copy-start(bf16[4,128,128]{2,1,0:T(8,128)(2,1)} %param.21) | copy-start | bytes 393220
  56.3 97.3 %all-gather.8.cloned.1.call-start = ((), (), s32[]{:S(2)}) async-start(), calls=%async_computation.2 | async-start | bytes 1310720 | tf_op jit(solution)/shard_map/all_gather | solution.py:14
  80.5 31.6 %collective-permute-start = (bf16[2048,256]{1,0:T(8,128)(2,1)}, bf16[2048,256]{1,0:T(8,128)(2,1)}, u32[]{:S(2)}, u32[]{:S(2)}) collective-permute-start(bf16[2048,256]{1,0:T(8,128)(2,1)} %all-gather.6.cloned.1.call-done), channel_id=1, source_target_pairs={{0,4},{4,8},{8,12},{12,16},{16,20},{20,24},{24,28},{28,32},{32,36}... | collective-permute-start | bytes 3145736 | tf_op jit(solution)/shard_map/ppermute | solution.py:10
  153.5 31.6 %collective-permute-start.1 = (bf16[2048,256]{1,0:T(8,128)(2,1)}, bf16[2048,256]{1,0:T(8,128)(2,1)}, u32[]{:S(2)}, u32[]{:S(2)}) collective-permute-start(bf16[2048,256]{1,0:T(8,128)(2,1)} %all-gather.8.cloned.1.call-done), channel_id=1, source_target_pairs={{0,4},{4,8},{8,12},{12,16},{16,20},{20,24},{24,28},{28,32},{32,36}... | collective-permute-start | bytes 3145736 | tf_op jit(solution)/shard_map/ppermute | solution.py:10
  201.6 3.4 %copy-start.1 = (bf16[4,256,128]{1,2,0:T(8,128)(2,1)S(1)}, bf16[4,256,128]{1,2,0:T(8,128)(2,1)}, u32[]{:S(2)}) copy-start(bf16[4,256,128]{1,2,0:T(8,128)(2,1)} %fusion.90) | copy-start | bytes 786436
Sparse Core Ops, SparseCore 0:
  9.8 26.4 all-gather.3
  56.4 24.0 all-gather.5
  132.2 21.2 all-gather.7
where the time goes:
time: 217 us
  waiting for transfers between devices  123 us (57%)
  local copies, waits for them, and re-layouts  37.3 us (17%)
  matrix products  28.3 us (13%)
  between operations  13.8 us (6%)
  other arithmetic  8.01 us (4%)
  starting transfers between devices  6.64 us (3%)
    all_gather x3, waiting for transfers between devices, collect(): return lax.all_gather(share, 'sub', axis=0, tiled=True)  65.1 us
    ppermute x2, waiting for transfers between devices, passed_along(): return lax.ppermute(x, axis, pairs)  56.7 us
    gather x3, local copies, waits for them, and re-layouts, shards(): picked = jnp.take(front_blocks, inner_index, axis=0)  21.6 us
    dot_general x3, matrix products, shards(): jnp.einsum('iab,ibc->iac', inner_inverse, inner_values, preferred_element...  18.1 us
    dot_general x3, matrix products, shards(): jnp.einsum('jab,jbc->jac', front_inverse, outer_values, preferred_element...  10.2 us
    gather x3, local copies, waits for them, and re-layouts, shards(): chosen = jnp.take(solved, outer_index, axis=0)  9.7 us
    ppermute x2, starting transfers between devices, passed_along(): return lax.ppermute(x, axis, pairs)  6.52 us
  transfers between devices with their start and end apart: 5, of which 5 were waited for; matrix products, arithmetic and copies ran while one was open for 4% of the time, Pallas kernels for 0%

commit v1 on v0

--- a/solution.py
+++ b/solution.py
@@ -2,6 +2,13 @@
 import jax.numpy as jnp
 from jax import lax
 from jax.sharding import PartitionSpec as P
+from jax.lax import all_to_all, psum
+
+
+def solve_slices(u, mesh_ax):
+    wide_out = all_to_all(jnp.stack([u for _ in range(psum(1, mesh_ax))]), mesh_ax, 0, 0)
+    reached = jnp.concatenate(wide_out, axis=0)
+    return reached
 
 
 def passed_along(x, axis, by):
@@ -11,7 +18,7 @@
 
 
 def collect(share):
-    return lax.all_gather(share, "sub", axis=0, tiled=True)
+    return solve_slices(share, "sub")
 
 
 def shards(

time: 217 us -> 185 us (0.85)
  waiting for transfers between devices: 123 us -> 64.5 us
  blocking collectives: 0 us -> 34.2 us
  between operations: 13.8 us -> 0.73 us
  starting transfers between devices: 6.64 us -> 10.5 us
  local copies, waits for them, and re-layouts: 37.3 us -> 40.7 us
  other arithmetic: 8.01 us -> 5.12 us
    all_gather x3 -> x0, waiting for transfers between devices: 65.1 us -> none  [collect(): return lax.all_gather(share, 'sub', axis=0, tiled=True)]
    all_to_all x0 -> x2, blocking collectives: none -> 34.2 us  [solve_slices(): all_to_all(jnp.stack([u for _ in range(psum(1, mesh_ax))]), mesh_ax, 0, 0)]
    all_to_all x0 -> x1, waiting for transfers between devices: none -> 7.52 us  [solve_slices(): all_to_all(jnp.stack([u for _ in range(psum(1, mesh_ax))]), mesh_ax, 0, 0)]
    all_to_all x0 -> x1, starting transfers between devices: none -> 4.87 us  [solve_slices(): all_to_all(jnp.stack([u for _ in range(psum(1, mesh_ax))]), mesh_ax, 0, 0)]
    another operation x0 -> x3, local copies, waits for them, and re-layouts: none -> 3.31 us  [solve_slices(): jnp.stack([u for _ in range(psum(1, mesh_ax))])]
  transfers between devices with their start and end apart: 5 -> 3, of which waited for: 5 -> 3; matrix products, arithmetic and copies ran while one was open for 4% -> 3% of each run, Pallas kernels for 0% -> 0%
where the time goes in v1:
time: 185 us; the launch traced here: 183 us
  waiting for transfers between devices  64.5 us (35%)
  local copies, waits for them, and re-layouts  40.7 us (22%)
  blocking collectives  34.2 us (18%)
  matrix products  27.5 us (15%)
  starting transfers between devices  10.5 us (6%)
  other arithmetic  5.12 us (3%)
    ppermute x2, waiting for transfers between devices, passed_along(): return lax.ppermute(x, axis, pairs)  56.9 us
    all_to_all x2, blocking collectives, solve_slices(): all_to_all(jnp.stack([u for _ in range(psum(1, mesh_ax))]), mesh_ax, 0, 0)  34.2 us
    gather x3, local copies, waits for them, and re-layouts, shards(): picked = jnp.take(front_blocks, inner_index, axis=0)  21.7 us
    dot_general x3, matrix products, shards(): jnp.einsum('iab,ibc->iac', inner_inverse, inner_values, preferred_element...  18.1 us
    gather x3, local copies, waits for them, and re-layouts, shards(): chosen = jnp.take(solved, outer_index, axis=0)  9.7 us
    dot_general x3, matrix products, shards(): jnp.einsum('jab,jbc->jac', front_inverse, outer_values, preferred_element...  9.46 us
    all_to_all x1, waiting for transfers between devices, solve_slices(): all_to_all(jnp.stack([u for _ in range(psum(1, mesh_ax))]), mesh_ax, 0, 0)  7.52 us
    ppermute x2, starting transfers between devices, passed_along(): return lax.ppermute(x, axis, pairs)  5.64 us
  transfers between devices with their start and end apart: 3, of which 3 were waited for; matrix products, arithmetic and copies ran while one was open for 3% of the time, Pallas kernels for 0%

profile of v1, /device:TPU:9, one launch (start us, length us, event | category | flops | bytes accessed | tf_op | source)
XLA Modules:
  0.0 183.3 jit_solution(7949904036880430782)
XLA Ops:
  0.6 0.0 copy-start
  0.7 2.2 %stack.6 = bf16[4,512,256]{2,1,0:T(8,128)(2,1)} broadcast(bf16[512,256]{1,0:T(8,128)(2,1)} %param.15), dimensions={1,2} | broadcast | bytes 1310720 | tf_op jit(solution)/shard_map/stack | solution.py:9
  2.9 4.9 %all-to-all-start = ((bf16[4,512,256]{2,1,0:T(8,128)(2,1)}), bf16[4,512,256]{2,1,0:T(8,128)(2,1)}, u32[]{:S(2)}, u32[]{:S(2)}) async-start(bf16[4,512,256]{2,1,0:T(8,128)(2,1)} %stack.6), calls=%async_computation | async-start | bytes 2097152 | tf_op jit(solution)/shard_map/all_to_all | solution.py:9
  7.8 0.1 reshape.142
  7.9 0.1 copy.18
  8.0 0.1 reshape.138
  8.1 2.0 %fusion.115 = (bf16[512,256]{1,0:T(8,128)(2,1)}, bf16[512,256]{1,0:T(8,128)(2,1)}, bf16[512,256]{1,0:T(8,128)(2,1)}) fusion(bf16[512,768]{1,0:T(8,128)(2,1)} %param.14), kind=kLoop, calls=%fused_computation.75 | loop fusion | bytes 1572864 | tf_op jit(solution)/shard_map/slice | solution.py:60
  10.1 0.1 copy.17
  10.2 3.6 %fusion.114 = (bf16[2048,256]{1,0:T(8,128)(2,1)}, bf16[2048,256]{1,0:T(8,128)(2,1)}, bf16[2048,256]{1,0:T(8,128)(2,1)}) fusion(bf16[2048,768]{1,0:T(8,128)(2,1)} %param.13), kind=kLoop, calls=%fused_computation.74 | loop fusion | bytes 6291456 | tf_op jit(solution)/shard_map/slice | solution.py:49
  13.8 7.5 %all-to-all-done = bf16[4,512,256]{2,1,0:T(8,128)(2,1)} async-done(((bf16[4,512,256]{2,1,0:T(8,128)(2,1)}), bf16[4,512,256]{2,1,0:T(8,128)(2,1)}, u32[]{:S(2)}, u32[]{:S(2)}) %all-to-all-start) | async-done | bytes 1048608 | tf_op jit(solution)/shard_map/all_to_all | solution.py:9
  21.3 7.2 %gather_fusion = bf16[96,128,256]{2,1,0:T(8,128)(2,1)} fusion(bf16[16,128,256]{2,1,0:T(8,128)(2,1)} %bitcast.1, s32[1024]{0:T(1024)S(1)} %pad_clamp_fusion.1), kind=kCustom, calls=%fused_computation.clone | custom fusion | bytes 12583296 | tf_op jit(solution)/shard_map/jit(_take)/gather | solution.py:45
  28.6 6.0 %fusion.45 = bf16[16,256,128]{1,2,0:T(8,128)(2,1)} fusion(bf16[16,128,128]{2,1,0:T(8,128)(2,1)} %param.18, bf16[16,128,256]{2,1,0:T(8,128)(2,1)} %bitcast.145, bf16[16,6,128,128]{3,2,1,0:T(8,128)(2,1)S(1)} %copy-done, bf16[16,6,128,256]{3,2,1,0:T(8,128)(2,1)} %bitcast.132, pred[16,6]{1,0:T(8,128)(4,1)S(1)} %copy.17), kind=kOutput, calls=%fused_computation.39 | convolution fusion | flops 944766976 | bytes 12058720 | tf_op jit(solution)/shard_map/iab,ibc->iac/dot_general | solution.py:53
  34.6 3.3 %gather_fusion.1 = bf16[32,128,256]{2,1,0:T(8,128)(2,1)} fusion(bf16[16,128,256]{2,1,0:T(8,128)(2,1)} %bitcast.125, s32[1024]{0:T(1024)S(1)} %pad_clamp_fusion), kind=kCustom, calls=%fused_computation.1.clone | custom fusion | bytes 4194432 | tf_op jit(solution)/shard_map/jit(_take)/gather | solution.py:56
  37.8 2.7 %fusion.90 = bf16[4,256,128]{1,2,0:T(8,128)(2,1)S(1)} fusion(bf16[4,128,128]{2,1,0:T(8,128)(2,1)S(1)} %copy-done.3, bf16[4,8,128,128]{3,2,1,0:T(8,128)(2,1)} %param.20, bf16[4,8,128,256]{3,2,1,0:T(8,128)(2,1)} %bitcast.135, pred[4,8]{1,0:T(4,128)(4,1)S(1)} %compare_and_fusion.1, bf16[4,128,256]{2,1,0:T(8,128)(2,1)} %bitcast.148), kind=kOutput, calls=%fused_computation.54 | convolution fusion | flops 303562752 | bytes 3801120 | tf_op jit(solution)/shard_map/jab,jbc->jac/dot_general | solution.py:64
  40.5 0.1 stack.14
  40.6 16.8 %all_to_all.15 = bf16[4,512,256]{2,1,0:T(8,128)(2,1)S(1)} all-to-all(bf16[4,512,256]{2,1,0:T(8,128)(2,1)S(1)} %stack.14), channel_id=1, replica_groups=mesh['slab'=64,'sub'=4] {'sub'}, dimensions={0} | all-to-all | bytes 2097152 | tf_op jit(solution)/shard_map/all_to_all | solution.py:9
  57.4 3.5 %collective-permute-start = (bf16[2048,256]{1,0:T(8,128)(2,1)S(1)}, bf16[2048,256]{1,0:T(8,128)(2,1)}, u32[]{:S(2)}, u32[]{:S(2)}) collective-permute-start(bf16[2048,256]{1,0:T(8,128)(2,1)S(1)} %bitcast.137), channel_id=1, source_target_pairs={{0,4},{4,8},{8,12},{12,16},{16,20},{20,24},{24,28},{28,32},{32,36}... | collective-permute-start | bytes 3145736 | tf_op jit(solution)/shard_map/ppermute | solution.py:17
  61.0 28.9 %collective-permute-done = bf16[2048,256]{1,0:T(8,128)(2,1)} collective-permute-done((bf16[2048,256]{1,0:T(8,128)(2,1)S(1)}, bf16[2048,256]{1,0:T(8,128)(2,1)}, u32[]{:S(2)}, u32[]{:S(2)}) %collective-permute-start) | collective-permute-done | bytes 1048608 | tf_op jit(solution)/shard_map/ppermute | solution.py:17
  89.8 7.2 %gather_fusion.2 = bf16[96,128,256]{2,1,0:T(8,128)(2,1)} fusion(bf16[16,128,256]{2,1,0:T(8,128)(2,1)} %bitcast.17, s32[1024]{0:T(1024)S(1)} %pad_clamp_fusion.1), kind=kCustom, calls=%fused_computation.2.clone | custom fusion | bytes 12583296 | tf_op jit(solution)/shard_map/jit(_take)/gather | solution.py:45
  97.0 6.1 %fusion.42 = bf16[16,256,128]{1,2,0:T(8,128)(2,1)} fusion(bf16[16,128,128]{2,1,0:T(8,128)(2,1)} %param.18, bf16[16,128,256]{2,1,0:T(8,128)(2,1)} %bitcast.144, bf16[16,6,128,128]{3,2,1,0:T(8,128)(2,1)S(1)} %copy-done, bf16[16,6,128,256]{3,2,1,0:T(8,128)(2,1)} %bitcast.133, pred[16,6]{1,0:T(8,128)(4,1)S(1)} %copy.17), kind=kOutput, calls=%fused_computation.38 | convolution fusion | flops 944766976 | bytes 12058720 | tf_op jit(solution)/shard_map/iab,ibc->iac/dot_general | solution.py:53
  103.1 3.2 %gather_fusion.3 = bf16[32,128,256]{2,1,0:T(8,128)(2,1)} fusion(bf16[16,128,256]{2,1,0:T(8,128)(2,1)} %bitcast.127, s32[1024]{0:T(1024)S(1)} %pad_clamp_fusion), kind=kCustom, calls=%fused_computation.4.clone | custom fusion | bytes 4194432 | tf_op jit(solution)/shard_map/jit(_take)/gather | solution.py:56
  106.3 3.4 %fusion.87 = bf16[4,256,128]{1,2,0:T(8,128)(2,1)} fusion(bf16[4,128,128]{2,1,0:T(8,128)(2,1)S(1)} %copy-done.3, bf16[4,8,128,128]{3,2,1,0:T(8,128)(2,1)} %param.20, bf16[4,8,128,256]{3,2,1,0:T(8,128)(2,1)} %bitcast.136, pred[4,8]{1,0:T(4,128)(4,1)S(1)} %compare_and_fusion.1, bf16[4,128,256]{2,1,0:T(8,128)(2,1)} %bitcast.147), kind=kOutput, calls=%fused_computation.53 | convolution fusion | flops 303562752 | bytes 3801120 | tf_op jit(solution)/shard_map/jab,jbc->jac/dot_general | solution.py:64
  109.7 1.0 stack.15
  110.8 17.4 %all_to_all.16 = bf16[4,512,256]{2,1,0:T(8,128)(2,1)S(1)} all-to-all(bf16[4,512,256]{2,1,0:T(8,128)(2,1)S(1)} %stack.15), channel_id=1, replica_groups=mesh['slab'=64,'sub'=4] {'sub'}, dimensions={0} | all-to-all | bytes 2097152 | tf_op jit(solution)/shard_map/all_to_all | solution.py:9
  128.2 2.1 %collective-permute-start.1 = (bf16[2048,256]{1,0:T(8,128)(2,1)S(1)}, bf16[2048,256]{1,0:T(8,128)(2,1)}, u32[]{:S(2)}, u32[]{:S(2)}) collective-permute-start(bf16[2048,256]{1,0:T(8,128)(2,1)S(1)} %bitcast.138), channel_id=1, source_target_pairs={{0,4},{4,8},{8,12},{12,16},{16,20},{20,24},{24,28},{28,32},{32,36}... | collective-permute-start | bytes 3145736 | tf_op jit(solution)/shard_map/ppermute | solution.py:17
  130.3 28.1 %collective-permute-done.1 = bf16[2048,256]{1,0:T(8,128)(2,1)} collective-permute-done((bf16[2048,256]{1,0:T(8,128)(2,1)S(1)}, bf16[2048,256]{1,0:T(8,128)(2,1)}, u32[]{:S(2)}, u32[]{:S(2)}) %collective-permute-start.1) | collective-permute-done | bytes 1048608 | tf_op jit(solution)/shard_map/ppermute | solution.py:17
  158.4 7.2 %gather_fusion.4 = bf16[96,128,256]{2,1,0:T(8,128)(2,1)} fusion(bf16[16,128,256]{2,1,0:T(8,128)(2,1)} %bitcast.33, s32[1024]{0:T(1024)S(1)} %pad_clamp_fusion.1), kind=kCustom, calls=%fused_computation.3.clone | custom fusion | bytes 12583296 | tf_op jit(solution)/shard_map/jit(_take)/gather | solution.py:45
  165.6 6.0 %fusion.39 = bf16[16,256,128]{1,2,0:T(8,128)(2,1)} fusion(bf16[16,128,128]{2,1,0:T(8,128)(2,1)} %param.18, bf16[16,128,256]{2,1,0:T(8,128)(2,1)} %bitcast.143, bf16[16,6,128,128]{3,2,1,0:T(8,128)(2,1)S(1)} %copy-done, bf16[16,6,128,256]{3,2,1,0:T(8,128)(2,1)} %bitcast.131, pred[16,6]{1,0:T(8,128)(4,1)S(1)} %copy.17), kind=kOutput, calls=%fused_computation.37 | convolution fusion | flops 944766976 | bytes 12058720 | tf_op jit(solution)/shard_map/iab,ibc->iac/dot_general | solution.py:53
  171.6 3.2 %gather_fusion.5 = bf16[32,128,256]{2,1,0:T(8,128)(2,1)} fusion(bf16[16,128,256]{2,1,0:T(8,128)(2,1)} %bitcast.129, s32[1024]{0:T(1024)S(1)} %pad_clamp_fusion), kind=kCustom, calls=%fused_computation.5.clone | custom fusion | bytes 4194432 | tf_op jit(solution)/shard_map/jit(_take)/gather | solution.py:56
  174.8 3.4 %fusion.84 = bf16[4,256,128]{1,2,0:T(8,128)(2,1)} fusion(bf16[4,128,128]{2,1,0:T(8,128)(2,1)S(1)} %copy-done.3, bf16[4,8,128,128]{3,2,1,0:T(8,128)(2,1)} %param.20, bf16[4,8,128,256]{3,2,1,0:T(8,128)(2,1)} %bitcast.134, pred[4,8]{1,0:T(4,128)(4,1)S(1)} %compare_and_fusion.1, bf16[4,128,256]{2,1,0:T(8,128)(2,1)} %bitcast.146), kind=kOutput, calls=%fused_computation.52 | convolution fusion | flops 303562752 | bytes 3801120 | tf_op jit(solution)/shard_map/jab,jbc->jac/dot_general | solution.py:64
  178.2 2.0 %pad_maximum_fusion.1 = bf16[512,768]{1,0:T(8,128)(2,1)} fusion(bf16[512,256]{1,0:T(8,128)(2,1)} %bitcast.149, bf16[512,256]{1,0:T(8,128)(2,1)} %bitcast.142, bf16[512,256]{1,0:T(8,128)(2,1)S(1)} %bitcast.140), kind=kLoop, calls=%fused_computation.58 | loop fusion | flops 2359296 | bytes 1572864 | tf_op jit(solution)/shard_map/concatenate | solution.py:73
  180.2 3.1 %pad_maximum_fusion = bf16[2048,768]{1,0:T(8,128)(2,1)} fusion(bf16[2048,256]{1,0:T(8,128)(2,1)} %bitcast.130, bf16[2048,256]{1,0:T(8,128)(2,1)} %bitcast.128, bf16[2048,256]{1,0:T(8,128)(2,1)} %bitcast.126), kind=kLoop, calls=%fused_computation.15 | loop fusion | flops 9437184 | bytes 6291456 | tf_op jit(solution)/shard_map/concatenate | solution.py:72
  (13 shorter events, 0.1 us)
Async XLA Ops:
  0.6 27.9 %copy-start = (bf16[16,6,128,128]{3,2,1,0:T(8,128)(2,1)S(1)}, bf16[16,6,128,128]{3,2,1,0:T(8,128)(2,1)}, u32[]{:S(2)}) copy-start(bf16[16,6,128,128]{3,2,1,0:T(8,128)(2,1)} %param.17) | copy-start | bytes 9437188
  0.6 7.1 %copy-start.1 = (s32[16,6]{0,1:T(8,128)S(1)}, s32[16,6]{0,1:T(8,128)}, u32[]{:S(2)}) copy-start(s32[16,6]{0,1:T(8,128)} %param.16) | copy-start | bytes 1156
  0.7 7.1 %copy-start.2 = (s32[4,8]{1,0:T(4,128)S(1)}, s32[4,8]{1,0:T(4,128)}, u32[]{:S(2)}) copy-start(s32[4,8]{1,0:T(4,128)} %param.19) | copy-start | bytes 388
  2.9 18.4 %all-to-all-start = ((bf16[4,512,256]{2,1,0:T(8,128)(2,1)}), bf16[4,512,256]{2,1,0:T(8,128)(2,1)}, u32[]{:S(2)}, u32[]{:S(2)}) async-start(bf16[4,512,256]{2,1,0:T(8,128)(2,1)} %stack.6), calls=%async_computation | async-start | bytes 2097152 | tf_op jit(solution)/shard_map/all_to_all | solution.py:9
  34.6 3.3 %copy-start.3 = (bf16[4,128,128]{2,1,0:T(8,128)(2,1)S(1)}, bf16[4,128,128]{2,1,0:T(8,128)(2,1)}, u32[]{:S(2)}) copy-start(bf16[4,128,128]{2,1,0:T(8,128)(2,1)} %param.21) | copy-start | bytes 393220
  57.4 32.4 %collective-permute-start = (bf16[2048,256]{1,0:T(8,128)(2,1)S(1)}, bf16[2048,256]{1,0:T(8,128)(2,1)}, u32[]{:S(2)}, u32[]{:S(2)}) collective-permute-start(bf16[2048,256]{1,0:T(8,128)(2,1)S(1)} %bitcast.137), channel_id=1, source_target_pairs={{0,4},{4,8},{8,12},{12,16},{16,20},{20,24},{24,28},{28,32},{32,36}... | collective-permute-start | bytes 3145736 | tf_op jit(solution)/shard_map/ppermute | solution.py:17
  128.2 30.2 %collective-permute-start.1 = (bf16[2048,256]{1,0:T(8,128)(2,1)S(1)}, bf16[2048,256]{1,0:T(8,128)(2,1)}, u32[]{:S(2)}, u32[]{:S(2)}) collective-permute-start(bf16[2048,256]{1,0:T(8,128)(2,1)S(1)} %bitcast.138), channel_id=1, source_target_pairs={{0,4},{4,8},{8,12},{12,16},{16,20},{20,24},{24,28},{28,32},{32,36}... | collective-permute-start | bytes 3145736 | tf_op jit(solution)/shard_map/ppermute | solution.py:17
